TPU v7x, 32 devices: a whole 2x2x4 slice. The times are simulated.
32 devices in a mesh: grp: 8 (over z, x), blk: 4 (over y, core).
Axes of the slice: x: 2, y: 2, z: 4, core: 2. Of those that a mesh axis runs over, the one named last changes fastest.
Arguments:
- raw_ints: bfloat16 [2048, 32, 512], P('grp', 'blk'), may hold values from -0.59765625 to 0.59765625
- metric: bfloat16 [2048, 2048], P(None, 'grp'), as said below
- occ_energy: float32 [32], replicated, may hold values from -2 to -0.3
- virt_energy: float32 [512], replicated, may hold values from 0.2 to 5
Outputs:
- density: float32 [2048, 32, 512], P(None, ('blk', 'grp'))
- pair_energy: float32 [32, 4], P(('blk', 'grp'))
Inputs may be any that keep to these rules, and one draw needn't show every extreme that they name: `metric`: Symmetric.
All inputs are finite; a program needn't handle non-finite values.
Results may differ from a plain program's by a relative error of at most 0.0033.
Values may be sent and summed in bfloat16 or wider, within the bound.
No kernel may reach another device: no remote copies, remote signals or barrier semaphores. Data moves between devices by JAX's collectives and lax.ppermute only.
A program may use at most 128 MiB of HBM per device.

v0:
```python
import functools

import jax
import jax.numpy as jnp
from jax import lax
from jax.experimental import pallas as pl
from jax.experimental.pallas import tpu as pltpu
from jax.sharding import PartitionSpec as P

VISITS = 4
GROUPS = 4
BF16, F32 = jnp.bfloat16, jnp.float32
BOTH = ("grp", "blk")
VMEM_CAP = 56 * 2**20
SMEM = pl.BlockSpec(memory_space=pltpu.SMEM)
VMEM = pl.BlockSpec(memory_space=pltpu.VMEM)
ANY = pl.BlockSpec(memory_space=pl.ANY)
GRP, QUARTER, SOURCE, ORBITAL = 0, 1, 2, 3


def params():
    return pltpu.CompilerParams(vmem_limit_bytes=VMEM_CAP)


def cost(flops, moved):
    return pl.CostEstimate(flops=flops, bytes_accessed=moved, transcendentals=0)


def swapped(value, axis, mask):
    pairs = [(source, source ^ mask) for source in range(lax.axis_size(axis))]
    return lax.ppermute(value, axis, pairs)


def forwarded(value):
    total = lax.axis_size(BOTH)
    pairs = [(p, (p + 2) % total if p % 2 == 0 else (p - 2) % total) for p in range(total)]
    return lax.ppermute(value, BOTH, pairs)


def table_of_integers():
    n_grp, n_blk = lax.axis_size("grp"), lax.axis_size("blk")
    total = n_grp * n_blk
    g, b = lax.axis_index("grp"), lax.axis_index("blk")
    place = g * n_blk + b
    source = jnp.where(place % 2 == 0, (place - 2) % total, (place + 2) % total) // n_blk
    slot = jnp.arange(8, dtype=jnp.int32)
    spot = slot - ORBITAL
    partner = jnp.where((place - spot) % 2 == 0, (place - spot) % total, (place + spot) % total)
    orbital = partner % n_blk * n_grp + partner // n_blk
    table = jnp.where(slot == GRP, g, jnp.where(slot == QUARTER, b % 4, jnp.where(slot == SOURCE, source, orbital)))
    return table.astype(jnp.int32)


def pack_kernel(n_grp, table_ref, metric_ref, out_ref, sems):
    chunk = metric_ref.shape[0] // n_grp // 4
    copies = []
    for j in range(n_grp // 2 + 1):
        row = (((table_ref[GRP] + j) % n_grp) * 4 + table_ref[QUARTER]) * chunk
        copies.append(
            pltpu.make_async_copy(
                metric_ref.at[pl.ds(pl.multiple_of(row, chunk), chunk), :],
                out_ref.at[pl.ds(j * chunk, chunk), :],
                sems.at[j],
            )
        )
        copies[-1].start()
    for copy in copies:
        copy.wait()


def pack(metric, table, n_grp):
    rows, cols = metric.shape
    count = n_grp // 2 + 1
    return pl.pallas_call(
        functools.partial(pack_kernel, n_grp),
        in_specs=[SMEM, ANY],
        out_specs=VMEM,
        out_shape=jax.ShapeDtypeStruct((count * (rows // n_grp // 4), cols), metric.dtype),
        scratch_shapes=[pltpu.SemaphoreType.DMA((count,))],
        name="pack",
    )(table, metric)


def unpack_kernel(n_grp, table_ref, *refs):
    parts, out_ref = refs[:-1], refs[-1]
    width = out_ref.shape[0] // n_grp
    chunk = width // 4
    g, q = table_ref[GRP], table_ref[QUARTER]

    def place(m, carry):
        for at, part in enumerate(parts):
            odd, dq = at % 2, at // 2
            s = g ^ (2 * m + odd)
            cols = pl.ds(pl.multiple_of(s * width, width), width)
            for j in range(n_grp // 2 + 1):
                a = (s + j) % n_grp
                rows = pl.ds(pl.multiple_of(a * width + (q ^ dq) * chunk, chunk), chunk)
                out_ref[rows, cols] = part[m, j * chunk : (j + 1) * chunk, :]
        return carry

    lax.fori_loop(0, n_grp // 2, place, 0)

    def mirror(s, carry):
        here = pl.ds(pl.multiple_of(s * width, width), width)
        for j in range(1, n_grp // 2):
            there = pl.ds(pl.multiple_of(((s + j) % n_grp) * width, width), width)
            out_ref[here, there] = out_ref[there, here].T
        return carry

    lax.fori_loop(0, n_grp, mirror, 0)


def unpack(parts, table, n_grp):
    width = parts[0].shape[2]
    size = n_grp * width
    return pl.pallas_call(
        functools.partial(unpack_kernel, n_grp),
        in_specs=[SMEM] + [VMEM] * len(parts),
        out_specs=VMEM,
        out_shape=jax.ShapeDtypeStruct((size, size), parts[0].dtype),
        compiler_params=params(),
        cost_estimate=cost(0, 4 * size * size),
        name="unpack",
    )(table, *parts)


def fit_kernel(which, has_base, partial, table_ref, metric_ref, *refs):
    refs = list(refs)
    base_ref = refs.pop(0) if has_base else None
    acc_ref = refs.pop()
    out_ref = refs.pop()
    groups = refs
    step = pl.program_id(0)
    per = groups[0].shape[0]
    low = table_ref[which] % per
    for at, group in enumerate(groups):

        @pl.when(step == at)
        def _():
            raw = jnp.concatenate([group[j ^ low] for j in range(per)], axis=0)
            part = jnp.dot(metric_ref[...], raw, preferred_element_type=F32)
            if at == 0 and has_base:
                part = part + base_ref[...]
            if at > 0:
                part = part + acc_ref[...]
            if at < len(groups) - 1:
                acc_ref[...] = part
            else:
                out_ref[...] = part.astype(out_ref.dtype)


def fit(metric, groups, table, which, first=0, base=None, partial=False):
    size = metric.shape[0]
    per, width, nv = groups[0].shape
    fixed = pl.BlockSpec((per, width, nv), lambda i, t: (0, 0, 0))
    whole = pl.BlockSpec((size, nv), lambda i, t: (0, 0))
    return pl.pallas_call(
        functools.partial(fit_kernel, which, base is not None, partial),
        grid_spec=pltpu.PrefetchScalarGridSpec(
            num_scalar_prefetch=1,
            grid=(len(groups),),
            in_specs=[pl.BlockSpec((size, per * width), lambda i, t: (0, (t[which] // per) ^ (i + first)))]
            + ([whole] if base is not None else [])
            + [fixed] * len(groups),
            out_specs=whole,
            scratch_shapes=[pltpu.VMEM((size, nv), F32)],
        ),
        out_shape=jax.ShapeDtypeStruct((size, nv), F32 if partial else BF16),
        compiler_params=params(),
        cost_estimate=cost(2 * size * per * width * nv * len(groups), 2 * size * per * width * len(groups)),
        name="fit",
    )(table, metric, *(() if base is None else (base,)), *groups)


def tilde_into(tilde_ref, amp_ref, coulomb_ref, esum, virt_ref):
    nv = amp_ref.shape[0]
    slab = 128
    cuts = range(0, nv, slab)
    for r in cuts:
        mine = jnp.broadcast_to(virt_ref[:, r : r + slab], (slab, slab)).T
        for c in cuts:
            denom = esum - mine - virt_ref[:, c : c + slab]
            amp_ref[r : r + slab, c : c + slab] = coulomb_ref[r : r + slab, c : c + slab] / denom
    energy = jnp.float32(0)
    for r in cuts:
        tilde = 2.0 * amp_ref[r : r + slab, :] - amp_ref[:, r : r + slab].T
        energy += jnp.sum(coulomb_ref[r : r + slab, :] * tilde)
        tilde_ref[r : r + slab, :] = tilde.astype(BF16)
    return energy


def pair_kernel(visits, n_old, has_base, dense, final, known, tiles, *refs):
    refs = list(refs)
    take = lambda count: [refs.pop(0) for _ in range(count)]
    table_ref, occ_ref, virt_ref, own_ref = take(4)
    new = take(len(visits))
    old, old_tilde = take(n_old), take(n_old)
    base_ref = take(1)[0] if has_base else None
    known_refs = take(len(known))
    energy_ref = take(1)[0]
    dens_ref = take(1)[0] if dense else None
    tildes = take(len(visits)) if not dense else None
    coulombs = take(len(visits))
    amp_ref = take(1)[0]
    if dense:
        tildes = take(len(visits))
    step = pl.program_id(0)

    @pl.when(step < tiles)
    def _():
        for other, coulomb in zip(new, coulombs):
            part = lax.dot_general(
                own_ref[...], other[...], (((0,), (0,)), ((), ())), preferred_element_type=F32
            )

            @pl.when(step == 0)
            def _():
                coulomb[...] = part

            @pl.when(step > 0)
            def _():
                coulomb[...] += part

    @pl.when(step == tiles - 1)
    def _():
        e_own = occ_ref[table_ref[ORBITAL]]
        for ref, (start, count) in zip(known_refs, known):
            for i in range(count):
                energy_ref[0, start + i] = ref[0, i]
        for at, visit in enumerate(visits):
            esum = e_own + occ_ref[table_ref[ORBITAL + visit]]
            energy = tilde_into(tildes[at], amp_ref, coulombs[at], esum, virt_ref)
            energy_ref[0, visit if final else at] = energy

    if dense:

        @pl.when(step >= tiles)
        def _():
            total = base_ref[...] if has_base else None
            for other, tilde in list(zip(old, old_tilde)) + list(zip(new, tildes)):
                part = lax.dot_general(
                    other[...], tilde[...], (((1,), (1,)), ((), ())), preferred_element_type=F32
                )
                total = part if total is None else total + part
            if final:
                lanes = dens_ref.shape[1]
                ways = total.shape[1] // lanes
                for c in range(ways):
                    dens_ref[pl.ds(c, total.shape[0], stride=ways), :] = total[:, c * lanes : (c + 1) * lanes]
            else:
                dens_ref[...] = total


def pairs(own, new, visits, table, occ, virt, old=(), old_tilde=(), base=None, dense=True, final=False, known=()):
    size, nv = own.shape
    tiles = 2
    rows = size // tiles
    n_new, n_old = len(new), len(old)
    first = pl.BlockSpec((rows, nv), lambda i: (jnp.minimum(i, tiles - 1), 0))
    second = pl.BlockSpec((rows, nv), lambda i: (jnp.maximum(i - tiles, 0), 0))
    twice = pl.BlockSpec((rows, nv), lambda i: (i % tiles, 0))
    square = pl.BlockSpec((nv, nv), lambda i: (0, 0))
    in_specs = [SMEM, SMEM, pl.BlockSpec((1, nv), lambda i: (0, 0)), first]
    in_specs += [twice if dense else first] * n_new + [second] * n_old + [square] * n_old
    args = [table, occ, virt, own, *new, *old, *old_tilde]
    if base is not None:
        in_specs.append(second)
        args.append(base)
    in_specs += [SMEM] * len(known)
    args += [energy for _, _, energy in known]
    out_specs = [SMEM]
    out_shape = [jax.ShapeDtypeStruct((1, VISITS if final else n_new), F32)]
    scratch = [pltpu.VMEM((nv, nv), F32)] * (n_new + 1)
    if dense:
        if final:
            ways = nv // 128
            out_specs.append(pl.BlockSpec((rows * ways, 128), lambda i: (jnp.maximum(i - tiles, 0), 0)))
            out_shape.append(jax.ShapeDtypeStruct((size * ways, 128), F32))
        else:
            out_specs.append(second)
            out_shape.append(jax.ShapeDtypeStruct((size, nv), F32))
        scratch += [pltpu.VMEM((nv, nv), BF16)] * n_new
    else:
        out_specs += [square] * n_new
        out_shape += [jax.ShapeDtypeStruct((nv, nv), BF16)] * n_new
    work = n_new + (n_new + n_old if dense else 0)
    return pl.pallas_call(
        functools.partial(
            pair_kernel,
            tuple(visits),
            n_old,
            base is not None,
            dense,
            final,
            tuple((start, count) for start, count, _ in known),
            tiles,
        ),
        grid=(2 * tiles if dense else tiles,),
        in_specs=in_specs,
        out_specs=out_specs,
        out_shape=out_shape,
        scratch_shapes=scratch,
        compiler_params=params(),
        cost_estimate=cost(2 * size * nv * nv * work, 8 * size * nv),
        name="pairs",
    )(*args)


def body(raw_ints, metric, occ_energy, virt_energy):
    n_grp = lax.axis_size("grp")
    per = n_grp // GROUPS
    g = lax.axis_index("grp")
    table = table_of_integers()

    mine = pack(metric, table, n_grp)
    even = jnp.stack([mine] + [swapped(mine, "grp", k) for k in range(2, n_grp, 2)])
    odd = swapped(even, "grp", 1)
    even_y = swapped(even, "blk", 2)
    odd_y = swapped(odd, "blk", 2)
    parts = [even, odd, swapped(even, "blk", 1), swapped(odd, "blk", 1), even_y, odd_y]
    parts += [swapped(even_y, "blk", 1), swapped(odd_y, "blk", 1)]
    full = unpack(parts, table, n_grp)

    by_orbital = lax.optimization_barrier(jnp.transpose(raw_ints, (1, 0, 2)))
    got = [lax.dynamic_index_in_dim(by_orbital, g ^ k, 0, keepdims=False) for k in range(n_grp)]
    got = got[:1] + [swapped(got[k], "grp", k) for k in range(1, n_grp)]
    groups = [jnp.stack(got[i * per : (i + 1) * per]) for i in range(GROUPS)]
    next_groups = [forwarded(group) for group in groups]

    own = fit(full, groups, table, GRP)
    mate = swapped(own, "blk", 1)
    some = fit(full, next_groups[:-1], table, SOURCE, partial=True)
    next_ = fit(full, next_groups[-1:], table, SOURCE, first=GROUPS - 1, base=some)
    next_mate = swapped(next_, "blk", 1)

    virt = virt_energy[None, :]
    energy_a, base = pairs(own, [own, mate], [0, 1], table, occ_energy, virt)
    energy_b, tilde_b = pairs(own, [next_], [2], table, occ_energy, virt, dense=False)
    energy, density = pairs(
        own,
        [next_mate],
        [3],
        table,
        occ_energy,
        virt,
        old=[next_],
        old_tilde=[tilde_b],
        base=base,
        final=True,
        known=[(0, 2, energy_a), (2, 1, energy_b)],
    )
    size, nv = own.shape
    return density.reshape(size, 1, nv), energy


def solution(mesh):
    in_specs = (P("grp", "blk", None), P(None, "grp"), P(), P())
    out_specs = (P(None, ("blk", "grp"), None), P(("blk", "grp"), None))
    return jax.shard_map(body, mesh=mesh, in_specs=in_specs, out_specs=out_specs, check_vma=False)
```

profile of v0, /device:TPU:17, one launch (start us, length us, event | category | flops | bytes accessed | tf_op | source)
XLA Modules:
  0.0 209.6 jit_solution(4795332715309897006)
XLA Ops:
  1.3 2.2 %pack.1 = bf16[320,256]{1,0:T(8,128)(2,1)} custom-call(s32[8]{0:T(128)} %compare_select_fusion.5.table_ref.refs_0_, bf16[2048,256]{1,0:T(8,128)(2,1)} %metric_ref.1), custom_call_target="tpu_custom_call" | custom-call | tf_op jit(solution)/shard_map/pack/pallas_call | solution.py:74
  3.8 3.2 %collective-permute-start.1 = (bf16[320,256]{1,0:T(8,128)(2,1)}, bf16[320,256]{1,0:T(8,128)(2,1)S(1)}, u32[]{:S(2)}, u32[]{:S(2)}) collective-permute-start(bf16[320,256]{1,0:T(8,128)(2,1)} %pack.1), channel_id=1, source_target_pairs={{0,16},{4,20},{8,24},{12,28},{16,0},{20,4},{24,8},{28,12},{1,17},{... | collective-permute-start | bytes 491528 | tf_op jit(solution)/shard_map/ppermute | solution.py:31
  7.0 8.2 %collective-permute-done.2 = bf16[320,256]{1,0:T(8,128)(2,1)S(1)} collective-permute-done((bf16[320,256]{1,0:T(8,128)(2,1)}, bf16[320,256]{1,0:T(8,128)(2,1)S(1)}, u32[]{:S(2)}, u32[]{:S(2)}) %collective-permute-start.2) | collective-permute-done | bytes 163872 | tf_op jit(solution)/shard_map/ppermute | solution.py:31
  15.2 2.5 %collective-permute-done.1 = bf16[320,256]{1,0:T(8,128)(2,1)S(1)} collective-permute-done((bf16[320,256]{1,0:T(8,128)(2,1)}, bf16[320,256]{1,0:T(8,128)(2,1)S(1)}, u32[]{:S(2)}, u32[]{:S(2)}) %collective-permute-start.1) | collective-permute-done | bytes 163872 | tf_op jit(solution)/shard_map/ppermute | solution.py:31
  20.0 2.3 %copy.9 = bf16[256,8,512]{2,0,1:T(8,128)(2,1)S(1)} copy(bf16[256,8,512]{2,1,0:T(8,128)(2,1)} %param.4) | data formatting | bytes 4194304 | tf_op args[0]
  23.6 10.1 %collective-permute-done.3.refs_1_ = bf16[4,320,256]{2,1,0:T(8,128)(2,1)S(1)} collective-permute-done((bf16[4,320,256]{2,1,0:T(8,128)(2,1)S(1)}, bf16[4,320,256]{2,1,0:T(8,128)(2,1)S(1)}, u32[]{:S(2)}, u32[]{:S(2)}) %collective-permute-start.3) | collective-permute-done | bytes 655392 | tf_op jit(solution)/shard_map/ppermute | solution.py:31
  36.5 2.7 %collective-permute-start.12 = (bf16[256,512]{1,0:T(8,128)(2,1)S(1)}, bf16[256,512]{1,0:T(8,128)(2,1)S(1)}, u32[]{:S(2)}, u32[]{:S(2)}) collective-permute-start(bf16[256,512]{1,0:T(8,128)(2,1)S(1)} %get-tuple-element.20), channel_id=1, source_target_pairs={{0,12},{4,8},{8,4},{12,0},{16,28},{20,24},{24,20},{28,16},{1,13},{... | collective-permute-start | bytes 786440 | tf_op jit(solution)/shard_map/ppermute | solution.py:31
  39.2 4.9 %collective-permute-done.10 = bf16[256,512]{1,0:T(8,128)(2,1)S(1)} collective-permute-done((bf16[256,512]{1,0:T(8,128)(2,1)S(1)}, bf16[256,512]{1,0:T(8,128)(2,1)S(1)}, u32[]{:S(2)}, u32[]{:S(2)}) %collective-permute-start.10) | collective-permute-done | bytes 262176 | tf_op jit(solution)/shard_map/ppermute | solution.py:31
  44.1 7.7 %collective-permute-start.14 = (bf16[256,512]{1,0:T(8,128)(2,1)S(1)}, bf16[256,512]{1,0:T(8,128)(2,1)S(1)}, u32[]{:S(2)}, u32[]{:S(2)}) collective-permute-start(bf16[256,512]{1,0:T(8,128)(2,1)S(1)} %get-tuple-element.18), channel_id=1, source_target_pairs={{0,20},{4,16},{8,28},{12,24},{16,4},{20,0},{24,12},{28,8},{1,21},{... | collective-permute-start | bytes 786440 | tf_op jit(solution)/shard_map/ppermute | solution.py:31
  53.9 13.6 %collective-permute-done.14 = bf16[256,512]{1,0:T(8,128)(2,1)S(1)} collective-permute-done((bf16[256,512]{1,0:T(8,128)(2,1)S(1)}, bf16[256,512]{1,0:T(8,128)(2,1)S(1)}, u32[]{:S(2)}, u32[]{:S(2)}) %collective-permute-start.14) | collective-permute-done | bytes 262176 | tf_op jit(solution)/shard_map/ppermute | solution.py:31
  68.0 5.0 %collective-permute-done.13 = bf16[256,512]{1,0:T(8,128)(2,1)S(1)} collective-permute-done((bf16[256,512]{1,0:T(8,128)(2,1)S(1)}, bf16[256,512]{1,0:T(8,128)(2,1)S(1)}, u32[]{:S(2)}, u32[]{:S(2)}) %collective-permute-start.13) | collective-permute-done | bytes 262176 | tf_op jit(solution)/shard_map/ppermute | solution.py:31
  74.8 12.1 %collective-permute-done.16 = bf16[256,512]{1,0:T(8,128)(2,1)S(1)} collective-permute-done((bf16[256,512]{1,0:T(8,128)(2,1)S(1)}, bf16[256,512]{1,0:T(8,128)(2,1)S(1)}, u32[]{:S(2)}, u32[]{:S(2)}) %collective-permute-start.16) | collective-permute-done | bytes 262176 | tf_op jit(solution)/shard_map/ppermute | solution.py:31
  88.5 32.7 %collective-permute-done.15 = bf16[256,512]{1,0:T(8,128)(2,1)S(1)} collective-permute-done((bf16[256,512]{1,0:T(8,128)(2,1)S(1)}, bf16[256,512]{1,0:T(8,128)(2,1)S(1)}, u32[]{:S(2)}, u32[]{:S(2)}) %collective-permute-start.15) | collective-permute-done | bytes 262176 | tf_op jit(solution)/shard_map/ppermute | solution.py:31
  121.4 2.9 %collective-permute-start.20 = (bf16[2,256,512]{2,1,0:T(8,128)(2,1)S(1)}, bf16[2,256,512]{2,1,0:T(8,128)(2,1)S(1)}, u32[]{:S(2)}, u32[]{:S(2)}) collective-permute-start(bf16[2,256,512]{2,1,0:T(8,128)(2,1)S(1)} %pad_maximum_fusion.4.refs_3_), channel_id=1, source_target_pairs={{0,2},{1,31},{2,4},{3,1},{4,6},{5,3},{6,8},{7,5},{8,10},{9,7},{10,... | collective-permute-start | bytes 1572872 | tf_op jit(solution)/shard_map/ppermute | solution.py:37
  125.2 8.9 %unpack.1.metric_ref = bf16[2048,2048]{1,0:T(8,128)(2,1)} custom-call(s32[8]{0:T(128)} %compare_select_fusion.5.table_ref.refs_0_, bf16[4,320,256]{2,1,0:T(8,128)(2,1)} %copy-done, bf16[4,320,256]{2,1,0:T(8,128)(2,1)} %copy-done.1, bf16[4,320,256]{2,1,0:T(8,128)(2,1)} %copy-done.4, bf16[4,320,256]{2,1,0:T(8,128)(2,1)} %copy-done.5, ...), custom_call_target="tpu_custom_call" | custom-call | bytes 16777216 | tf_op jit(solution)/shard_map/unpack/pallas_call | solution.py:116
  134.1 9.7 %fit.3.refs_3_.refs_4_ = bf16[2048,512]{1,0:T(8,128)(2,1)} custom-call(s32[8]{0:T(128)} %compare_select_fusion.5.table_ref.refs_0_, bf16[2048,2048]{1,0:T(8,128)(2,1)} %unpack.1.metric_ref, bf16[2,256,512]{2,1,0:T(8,128)(2,1)} %pad_maximum_fusion.1.refs_0_, bf16[2,256,512]{2,1,0:T(8,128)(2,1)} %copy-done.13, bf16[2,256,512]{2,1,0:T(8,128)(2,1)} %copy-done.12, ...), custom_call_target="tpu_custom_call" | custom-call | flops 4294967296 | bytes 8388608 | tf_op jit(solution)/shard_map/fit/pallas_call | solution.py:157
  143.9 7.9 %collective-permute-done.17.refs_0_ = bf16[2,256,512]{2,1,0:T(8,128)(2,1)S(1)} collective-permute-done((bf16[2,256,512]{2,1,0:T(8,128)(2,1)}, bf16[2,256,512]{2,1,0:T(8,128)(2,1)S(1)}, u32[]{:S(2)}, u32[]{:S(2)}) %collective-permute-start.17) | collective-permute-done | bytes 524320 | tf_op jit(solution)/shard_map/ppermute | solution.py:37
  151.8 5.6 %collective-permute-done.18.refs_1_ = bf16[2,256,512]{2,1,0:T(8,128)(2,1)S(1)} collective-permute-done((bf16[2,256,512]{2,1,0:T(8,128)(2,1)S(1)}, bf16[2,256,512]{2,1,0:T(8,128)(2,1)S(1)}, u32[]{:S(2)}, u32[]{:S(2)}) %collective-permute-start.18) | collective-permute-done | bytes 524320 | tf_op jit(solution)/shard_map/ppermute | solution.py:37
  157.4 5.6 %collective-permute-done.19.refs_2_ = bf16[2,256,512]{2,1,0:T(8,128)(2,1)S(1)} collective-permute-done((bf16[2,256,512]{2,1,0:T(8,128)(2,1)S(1)}, bf16[2,256,512]{2,1,0:T(8,128)(2,1)S(1)}, u32[]{:S(2)}, u32[]{:S(2)}) %collective-permute-start.19) | collective-permute-done | bytes 524320 | tf_op jit(solution)/shard_map/ppermute | solution.py:37
  163.9 8.8 %fit.4.refs_0_ = f32[2048,512]{1,0:T(8,128)} custom-call(s32[8]{0:T(128)} %compare_select_fusion.5.table_ref.refs_0_, bf16[2048,2048]{1,0:T(8,128)(2,1)} %unpack.1.metric_ref, bf16[2,256,512]{2,1,0:T(8,128)(2,1)} %copy-done.8, bf16[2,256,512]{2,1,0:T(8,128)(2,1)} %copy-done.9, bf16[2,256,512]{2,1,0:T(8,128)(2,1)} %copy-done.10), custom_call_target="tpu_custom_call" | custom-call | flops 3221225472 | bytes 6291456 | tf_op jit(solution)/shard_map/fit/pallas_call | solution.py:157
  173.5 6.3 %fit.5.refs_4_.refs_5_ = bf16[2048,512]{1,0:T(8,128)(2,1)} custom-call(s32[8]{0:T(128)} %compare_select_fusion.5.table_ref.refs_0_, bf16[2048,2048]{1,0:T(8,128)(2,1)} %unpack.1.metric_ref, f32[2048,512]{1,0:T(8,128)} %fit.4.refs_0_, bf16[2,256,512]{2,1,0:T(8,128)(2,1)} %copy-done.11), custom_call_target="tpu_custom_call" | custom-call | flops 1073741824 | bytes 2097152 | tf_op jit(solution)/shard_map/fit/pallas_call | solution.py:157
  179.8 4.8 %pairs.3 = (f32[1,1]{1,0:T(1,128)}, bf16[512,512]{1,0:T(8,128)(2,1)}) custom-call(s32[8]{0:T(128)} %compare_select_fusion.5.table_ref.refs_0_, f32[32]{0:T(128)} %refs_1_.5, f32[1,512]{1,0:T(1,128)} %bitcast.42, bf16[2048,512]{1,0:T(8,128)(2,1)} %fit.3.refs_3_.refs_4_, bf16[2048,512]{1,0:T(8,128)(2,1)} %fit.5.refs_4_.refs_5_), custom_call_target="tpu_custom_call" | custom-call | flops 1073741824 | bytes 8388608 | tf_op jit(solution)/shard_map/pairs/pallas_call | solution.py:287
  186.0 11.3 %pairs.4 = (f32[1,2]{1,0:T(1,128)}, f32[2048,512]{1,0:T(8,128)}) custom-call(s32[8]{0:T(128)} %compare_select_fusion.5.table_ref.refs_0_, f32[32]{0:T(128)} %refs_1_.5, f32[1,512]{1,0:T(1,128)} %bitcast.43, bf16[2048,512]{1,0:T(8,128)(2,1)} %fit.3.refs_3_.refs_4_, bf16[2048,512]{1,0:T(8,128)(2,1)} %fit.3.refs_3_.refs_4_, bf16[2048,512]{1,0:T(8,128)(2,1)} %copy-done.15), custom_call_target="tpu_custom_call" | custom-call | flops 4294967296 | bytes 8388608 | tf_op jit(solution)/shard_map/pairs/pallas_call | solution.py:287
  198.7 10.9 %pairs.5 = (f32[1,4]{1,0:T(1,128)}, f32[8192,128]{1,0:T(8,128)}) custom-call(s32[8]{0:T(128)} %compare_select_fusion.5.table_ref.refs_0_, f32[32]{0:T(128)} %refs_1_.5, f32[1,512]{1,0:T(1,128)} %bitcast.44, bf16[2048,512]{1,0:T(8,128)(2,1)} %fit.3.refs_3_.refs_4_, bf16[2048,512]{1,0:T(8,128)(2,1)} %copy-done.16, bf16[2048,512]{1,0:T(8,128)(2,1)} %fit.5.refs_4_.refs_5_, ...), custom_call_target="tpu_custom_call" | custom-call | flops 3221225472 | bytes 8388608 | tf_op jit(solution)/shard_map/pairs/pallas_call | solution.py:287
  (72 shorter events, 18.5 us)
Async XLA Ops:
  3.5 11.7 %collective-permute-start.2 = (bf16[320,256]{1,0:T(8,128)(2,1)}, bf16[320,256]{1,0:T(8,128)(2,1)S(1)}, u32[]{:S(2)}, u32[]{:S(2)}) collective-permute-start(bf16[320,256]{1,0:T(8,128)(2,1)} %pack.1), channel_id=1, source_target_pairs={{0,24},{4,28},{8,16},{12,20},{16,8},{20,12},{24,0},{28,4},{1,25},{... | collective-permute-start | bytes 491528 | tf_op jit(solution)/shard_map/ppermute | solution.py:31
  3.8 13.9 %collective-permute-start.1 = (bf16[320,256]{1,0:T(8,128)(2,1)}, bf16[320,256]{1,0:T(8,128)(2,1)S(1)}, u32[]{:S(2)}, u32[]{:S(2)}) collective-permute-start(bf16[320,256]{1,0:T(8,128)(2,1)} %pack.1), channel_id=1, source_target_pairs={{0,16},{4,20},{8,24},{12,28},{16,0},{20,4},{24,8},{28,12},{1,17},{... | collective-permute-start | bytes 491528 | tf_op jit(solution)/shard_map/ppermute | solution.py:31
  7.0 10.7 %collective-permute-start = (bf16[320,256]{1,0:T(8,128)(2,1)}, bf16[320,256]{1,0:T(8,128)(2,1)S(1)}, u32[]{:S(2)}, u32[]{:S(2)}) collective-permute-start(bf16[320,256]{1,0:T(8,128)(2,1)} %pack.1), channel_id=1, source_target_pairs={{0,8},{4,12},{8,0},{12,4},{16,24},{20,28},{24,16},{28,20},{1,9},{5... | collective-permute-start | bytes 491528 | tf_op jit(solution)/shard_map/ppermute | solution.py:31
  18.7 15.0 %collective-permute-start.3 = (bf16[4,320,256]{2,1,0:T(8,128)(2,1)S(1)}, bf16[4,320,256]{2,1,0:T(8,128)(2,1)S(1)}, u32[]{:S(2)}, u32[]{:S(2)}) collective-permute-start(bf16[4,320,256]{2,1,0:T(8,128)(2,1)S(1)} %pad_maximum_fusion.refs_0_), channel_id=1, source_target_pairs={{0,4},{4,0},{8,12},{12,8},{16,20},{20,16},{24,28},{28,24},{1,5},{5... | collective-permute-start | bytes 1966088 | tf_op jit(solution)/shard_map/ppermute | solution.py:31
  22.3 50.9 %collective-permute-start.6 = (bf16[4,320,256]{2,1,0:T(8,128)(2,1)S(1)}, bf16[4,320,256]{2,1,0:T(8,128)(2,1)S(1)}, u32[]{:S(2)}, u32[]{:S(2)}) collective-permute-start(bf16[4,320,256]{2,1,0:T(8,128)(2,1)S(1)} %pad_maximum_fusion.refs_0_), channel_id=1, source_target_pairs={{0,2},{1,3},{2,0},{3,1},{4,6},{5,7},{6,4},{7,5},{8,10},{9,11},{10,... | collective-permute-start | bytes 1966088 | tf_op jit(solution)/shard_map/ppermute | solution.py:31
  33.7 41.0 %collective-permute-start.7 = (bf16[4,320,256]{2,1,0:T(8,128)(2,1)S(1)}, bf16[4,320,256]{2,1,0:T(8,128)(2,1)S(1)}, u32[]{:S(2)}, u32[]{:S(2)}) collective-permute-start(bf16[4,320,256]{2,1,0:T(8,128)(2,1)S(1)} %collective-permute-done.3.refs_1_), channel_id=1, source_target_pairs={{0,2},{1,3},{2,0},{3,1},{4,6},{5,7},{6,4},{7,5},{8,10},{9,11},{10,... | collective-permute-start | bytes 1966088 | tf_op jit(solution)/shard_map/ppermute | solution.py:31
  35.2 8.9 %collective-permute-start.10 = (bf16[256,512]{1,0:T(8,128)(2,1)S(1)}, bf16[256,512]{1,0:T(8,128)(2,1)S(1)}, u32[]{:S(2)}, u32[]{:S(2)}) collective-permute-start(bf16[256,512]{1,0:T(8,128)(2,1)S(1)} %get-tuple-element.22), channel_id=1, source_target_pairs={{0,4},{4,0},{8,12},{12,8},{16,20},{20,16},{24,28},{28,24},{1,5},{5... | collective-permute-start | bytes 786440 | tf_op jit(solution)/shard_map/ppermute | solution.py:31
  36.5 15.4 %collective-permute-start.12 = (bf16[256,512]{1,0:T(8,128)(2,1)S(1)}, bf16[256,512]{1,0:T(8,128)(2,1)S(1)}, u32[]{:S(2)}, u32[]{:S(2)}) collective-permute-start(bf16[256,512]{1,0:T(8,128)(2,1)S(1)} %get-tuple-element.20), channel_id=1, source_target_pairs={{0,12},{4,8},{8,4},{12,0},{16,28},{20,24},{24,20},{28,16},{1,13},{... | collective-permute-start | bytes 786440 | tf_op jit(solution)/shard_map/ppermute | solution.py:31
  39.2 12.7 %collective-permute-start.11 = (bf16[256,512]{1,0:T(8,128)(2,1)S(1)}, bf16[256,512]{1,0:T(8,128)(2,1)S(1)}, u32[]{:S(2)}, u32[]{:S(2)}) collective-permute-start(bf16[256,512]{1,0:T(8,128)(2,1)S(1)} %get-tuple-element.21), channel_id=1, source_target_pairs={{0,8},{4,12},{8,0},{12,4},{16,24},{20,28},{24,16},{28,20},{1,9},{5... | collective-permute-start | bytes 786440 | tf_op jit(solution)/shard_map/ppermute | solution.py:31
  44.1 23.3 %collective-permute-start.14 = (bf16[256,512]{1,0:T(8,128)(2,1)S(1)}, bf16[256,512]{1,0:T(8,128)(2,1)S(1)}, u32[]{:S(2)}, u32[]{:S(2)}) collective-permute-start(bf16[256,512]{1,0:T(8,128)(2,1)S(1)} %get-tuple-element.18), channel_id=1, source_target_pairs={{0,20},{4,16},{8,28},{12,24},{16,4},{20,0},{24,12},{28,8},{1,21},{... | collective-permute-start | bytes 786440 | tf_op jit(solution)/shard_map/ppermute | solution.py:31
  51.9 21.2 %collective-permute-start.13 = (bf16[256,512]{1,0:T(8,128)(2,1)S(1)}, bf16[256,512]{1,0:T(8,128)(2,1)S(1)}, u32[]{:S(2)}, u32[]{:S(2)}) collective-permute-start(bf16[256,512]{1,0:T(8,128)(2,1)S(1)} %get-tuple-element.19), channel_id=1, source_target_pairs={{0,16},{4,20},{8,24},{12,28},{16,0},{20,4},{24,8},{28,12},{1,17},{... | collective-permute-start | bytes 786440 | tf_op jit(solution)/shard_map/ppermute | solution.py:31
  51.9 69.2 %collective-permute-start.4 = (bf16[4,320,256]{2,1,0:T(8,128)(2,1)S(1)}, bf16[4,320,256]{2,1,0:T(8,128)(2,1)S(1)}, u32[]{:S(2)}, u32[]{:S(2)}) collective-permute-start(bf16[4,320,256]{2,1,0:T(8,128)(2,1)S(1)} %pad_maximum_fusion.refs_0_), channel_id=1, source_target_pairs={{0,1},{1,0},{2,3},{3,2},{4,5},{5,4},{6,7},{7,6},{8,9},{9,8},{10,11... | collective-permute-start | bytes 1966088 | tf_op jit(solution)/shard_map/ppermute | solution.py:31
  67.5 53.7 %collective-permute-start.5 = (bf16[4,320,256]{2,1,0:T(8,128)(2,1)S(1)}, bf16[4,320,256]{2,1,0:T(8,128)(2,1)S(1)}, u32[]{:S(2)}, u32[]{:S(2)}) collective-permute-start(bf16[4,320,256]{2,1,0:T(8,128)(2,1)S(1)} %collective-permute-done.3.refs_1_), channel_id=1, source_target_pairs={{0,1},{1,0},{2,3},{3,2},{4,5},{5,4},{6,7},{7,6},{8,9},{9,8},{10,11... | collective-permute-start | bytes 1966088 | tf_op jit(solution)/shard_map/ppermute | solution.py:31
  73.1 13.9 %collective-permute-start.16 = (bf16[256,512]{1,0:T(8,128)(2,1)S(1)}, bf16[256,512]{1,0:T(8,128)(2,1)S(1)}, u32[]{:S(2)}, u32[]{:S(2)}) collective-permute-start(bf16[256,512]{1,0:T(8,128)(2,1)S(1)} %get-tuple-element.17), channel_id=1, source_target_pairs={{0,28},{4,24},{8,20},{12,16},{16,12},{20,8},{24,4},{28,0},{1,29},{... | collective-permute-start | bytes 786440 | tf_op jit(solution)/shard_map/ppermute | solution.py:31
  73.2 48.2 %copy-start.2 = (bf16[4,320,256]{2,1,0:T(8,128)(2,1)}, bf16[4,320,256]{2,1,0:T(8,128)(2,1)S(1)}, u32[]{:S(2)}) copy-start(bf16[4,320,256]{2,1,0:T(8,128)(2,1)S(1)} %collective-permute-done.6.refs_4_) | copy-start | bytes 1966084
  73.2 48.2 %collective-permute-start.8 = (bf16[4,320,256]{2,1,0:T(8,128)(2,1)S(1)}, bf16[4,320,256]{2,1,0:T(8,128)(2,1)S(1)}, u32[]{:S(2)}, u32[]{:S(2)}) collective-permute-start(bf16[4,320,256]{2,1,0:T(8,128)(2,1)S(1)} %collective-permute-done.6.refs_4_), channel_id=1, source_target_pairs={{0,1},{1,0},{2,3},{3,2},{4,5},{5,4},{6,7},{7,6},{8,9},{9,8},{10,11... | collective-permute-start | bytes 1966088 | tf_op jit(solution)/shard_map/ppermute | solution.py:31
  74.7 49.5 %collective-permute-start.9 = (bf16[4,320,256]{2,1,0:T(8,128)(2,1)S(1)}, bf16[4,320,256]{2,1,0:T(8,128)(2,1)S(1)}, u32[]{:S(2)}, u32[]{:S(2)}) collective-permute-start(bf16[4,320,256]{2,1,0:T(8,128)(2,1)S(1)} %collective-permute-done.7.refs_5_), channel_id=1, source_target_pairs={{0,1},{1,0},{2,3},{3,2},{4,5},{5,4},{6,7},{7,6},{8,9},{9,8},{10,11... | collective-permute-start | bytes 1966088 | tf_op jit(solution)/shard_map/ppermute | solution.py:31
  87.0 34.1 %collective-permute-start.15 = (bf16[256,512]{1,0:T(8,128)(2,1)S(1)}, bf16[256,512]{1,0:T(8,128)(2,1)S(1)}, u32[]{:S(2)}, u32[]{:S(2)}) collective-permute-start(bf16[256,512]{1,0:T(8,128)(2,1)S(1)} %get-tuple-element.16), channel_id=1, source_target_pairs={{0,24},{4,28},{8,16},{12,20},{16,8},{20,12},{24,0},{28,4},{1,25},{... | collective-permute-start | bytes 786440 | tf_op jit(solution)/shard_map/ppermute | solution.py:31
  121.1 30.7 %collective-permute-start.17 = (bf16[2,256,512]{2,1,0:T(8,128)(2,1)}, bf16[2,256,512]{2,1,0:T(8,128)(2,1)S(1)}, u32[]{:S(2)}, u32[]{:S(2)}) collective-permute-start(bf16[2,256,512]{2,1,0:T(8,128)(2,1)} %pad_maximum_fusion.1.refs_0_), channel_id=1, source_target_pairs={{0,2},{1,31},{2,4},{3,1},{4,6},{5,3},{6,8},{7,5},{8,10},{9,7},{10,... | collective-permute-start | bytes 1572872 | tf_op jit(solution)/shard_map/ppermute | solution.py:37
  121.1 36.3 %collective-permute-start.18 = (bf16[2,256,512]{2,1,0:T(8,128)(2,1)S(1)}, bf16[2,256,512]{2,1,0:T(8,128)(2,1)S(1)}, u32[]{:S(2)}, u32[]{:S(2)}) collective-permute-start(bf16[2,256,512]{2,1,0:T(8,128)(2,1)S(1)} %pad_maximum_fusion.2.refs_1_), channel_id=1, source_target_pairs={{0,2},{1,31},{2,4},{3,1},{4,6},{5,3},{6,8},{7,5},{8,10},{9,7},{10,... | collective-permute-start | bytes 1572872 | tf_op jit(solution)/shard_map/ppermute | solution.py:37
  121.2 41.9 %collective-permute-start.19 = (bf16[2,256,512]{2,1,0:T(8,128)(2,1)S(1)}, bf16[2,256,512]{2,1,0:T(8,128)(2,1)S(1)}, u32[]{:S(2)}, u32[]{:S(2)}) collective-permute-start(bf16[2,256,512]{2,1,0:T(8,128)(2,1)S(1)} %pad_maximum_fusion.3.refs_2_), channel_id=1, source_target_pairs={{0,2},{1,31},{2,4},{3,1},{4,6},{5,3},{6,8},{7,5},{8,10},{9,7},{10,... | collective-permute-start | bytes 1572872 | tf_op jit(solution)/shard_map/ppermute | solution.py:37
  121.4 51.3 %collective-permute-start.20 = (bf16[2,256,512]{2,1,0:T(8,128)(2,1)S(1)}, bf16[2,256,512]{2,1,0:T(8,128)(2,1)S(1)}, u32[]{:S(2)}, u32[]{:S(2)}) collective-permute-start(bf16[2,256,512]{2,1,0:T(8,128)(2,1)S(1)} %pad_maximum_fusion.4.refs_3_), channel_id=1, source_target_pairs={{0,2},{1,31},{2,4},{3,1},{4,6},{5,3},{6,8},{7,5},{8,10},{9,7},{10,... | collective-permute-start | bytes 1572872 | tf_op jit(solution)/shard_map/ppermute | solution.py:37
  143.8 40.9 %collective-permute-start.22 = (bf16[2048,512]{1,0:T(8,128)(2,1)}, bf16[2048,512]{1,0:T(8,128)(2,1)S(1)}, u32[]{:S(2)}, u32[]{:S(2)}) collective-permute-start(bf16[2048,512]{1,0:T(8,128)(2,1)} %fit.3.refs_3_.refs_4_), channel_id=1, source_target_pairs={{0,1},{1,0},{2,3},{3,2},{4,5},{5,4},{6,7},{7,6},{8,9},{9,8},{10,11... | collective-permute-start | bytes 6291464 | tf_op jit(solution)/shard_map/ppermute | solution.py:31
  179.8 17.4 %collective-permute-start.21 = (bf16[2048,512]{1,0:T(8,128)(2,1)}, bf16[2048,512]{1,0:T(8,128)(2,1)S(1)}, u32[]{:S(2)}, u32[]{:S(2)}) collective-permute-start(bf16[2048,512]{1,0:T(8,128)(2,1)} %fit.5.refs_4_.refs_5_), channel_id=1, source_target_pairs={{0,1},{1,0},{2,3},{3,2},{4,5},{5,4},{6,7},{7,6},{8,9},{9,8},{10,11... | collective-permute-start | bytes 6291464 | tf_op jit(solution)/shard_map/ppermute | solution.py:31
  (16 other events, 248.8 us)
where the time goes:
time: 210 us
  waiting for transfers between devices  108 us (51%)
  Pallas kernels  62.9 us (30%)
  starting transfers between devices  27 us (13%)
  local copies, waits for them, and re-layouts  7.73 us (4%)
  other arithmetic  2.59 us (1%)
    ppermute x19, waiting for transfers between devices, swapped(): return lax.ppermute(value, axis, pairs)  89.2 us
    pallas_call x3, Pallas kernels, pairs(): pl.pallas_call(functools.partial(pair_kernel, tuple(visits), n_old, base...  27 us
    pallas_call x3, Pallas kernels, fit(): pl.pallas_call(functools.partial(fit_kernel, which, base is not None, par...  24.8 us
    ppermute x19, starting transfers between devices, swapped(): return lax.ppermute(value, axis, pairs)  24 us
    ppermute x4, waiting for transfers between devices, forwarded(): return lax.ppermute(value, BOTH, pairs)  19.2 us
    pallas_call x1, Pallas kernels, unpack(): pl.pallas_call(functools.partial(unpack_kernel, n_grp), in_specs=[SMEM] +...  8.87 us
    unnamed x35, local copies, waits for them, and re-layouts  7.52 us
  transfers between devices with their start and end apart: 23, of which 11 were waited for; matrix products, arithmetic and copies ran while one was open for 2% of the time, Pallas kernels for 24%

commit v1 on v0

v1 whole, which is shorter than its diff:
```python
import functools

import jax
import jax.numpy as jnp
from jax import lax
from jax.experimental import pallas as pl
from jax.experimental.pallas import tpu as pltpu
from jax.sharding import PartitionSpec as P

VISITS = 4
GROUPS = 4
BF16, F32 = jnp.bfloat16, jnp.float32
BOTH = ("grp", "blk")
VMEM_CAP = 16 * 2**20
TILE = 512
SMEM = pl.BlockSpec(memory_space=pltpu.SMEM)
VMEM = pl.BlockSpec(memory_space=pltpu.VMEM)
ANY = pl.BlockSpec(memory_space=pl.ANY)
GRP, QUARTER, SOURCE, ORBITAL = 0, 1, 2, 3


def params():
    return pltpu.CompilerParams(vmem_limit_bytes=VMEM_CAP)


def cost(flops, moved):
    return pl.CostEstimate(flops=flops, bytes_accessed=moved, transcendentals=0)


def swapped(value, axis, mask):
    pairs = [(source, source ^ mask) for source in range(lax.axis_size(axis))]
    return lax.ppermute(value, axis, pairs)


def forwarded(value):
    total = lax.axis_size(BOTH)
    pairs = [(p, (p + 2) % total if p % 2 == 0 else (p - 2) % total) for p in range(total)]
    return lax.ppermute(value, BOTH, pairs)


def table_of_integers():
    n_grp, n_blk = lax.axis_size("grp"), lax.axis_size("blk")
    total = n_grp * n_blk
    g, b = lax.axis_index("grp"), lax.axis_index("blk")
    place = g * n_blk + b
    source = jnp.where(place % 2 == 0, (place - 2) % total, (place + 2) % total) // n_blk
    slot = jnp.arange(8, dtype=jnp.int32)
    spot = slot - ORBITAL
    partner = jnp.where((place - spot) % 2 == 0, (place - spot) % total, (place + spot) % total)
    orbital = partner % n_blk * n_grp + partner // n_blk
    table = jnp.where(slot == GRP, g, jnp.where(slot == QUARTER, b % 4, jnp.where(slot == SOURCE, source, orbital)))
    return table.astype(jnp.int32)


def pack_kernel(n_grp, table_ref, metric_ref, out_ref, sems):
    chunk = metric_ref.shape[0] // n_grp // 4
    copies = []
    for j in range(n_grp // 2 + 1):
        row = (((table_ref[GRP] + j) % n_grp) * 4 + table_ref[QUARTER]) * chunk
        copies.append(
            pltpu.make_async_copy(
                metric_ref.at[pl.ds(pl.multiple_of(row, chunk), chunk), :],
                out_ref.at[pl.ds(j * chunk, chunk), :],
                sems.at[j],
            )
        )
        copies[-1].start()
    for copy in copies:
        copy.wait()


def pack(metric, table, n_grp):
    rows, cols = metric.shape
    count = n_grp // 2 + 1
    return pl.pallas_call(
        functools.partial(pack_kernel, n_grp),
        in_specs=[SMEM, ANY],
        out_specs=VMEM,
        out_shape=jax.ShapeDtypeStruct((count * (rows // n_grp // 4), cols), metric.dtype),
        scratch_shapes=[pltpu.SemaphoreType.DMA((count,))],
        name="pack",
    )(table, metric)


def unpack_kernel(n_grp, table_ref, *refs):
    parts, out_ref = refs[:-1], refs[-1]
    width = out_ref.shape[0] // n_grp
    chunk = width // 4
    g, q = table_ref[GRP], table_ref[QUARTER]

    def place(m, carry):
        for at, part in enumerate(parts):
            odd, dq = at % 2, at // 2
            s = g ^ (2 * m + odd)
            cols = pl.ds(pl.multiple_of(s * width, width), width)
            for j in range(n_grp // 2 + 1):
                a = (s + j) % n_grp
                rows = pl.ds(pl.multiple_of(a * width + (q ^ dq) * chunk, chunk), chunk)
                out_ref[rows, cols] = part[m, j * chunk : (j + 1) * chunk, :]
        return carry

    lax.fori_loop(0, n_grp // 2, place, 0)

    def mirror(s, carry):
        here = pl.ds(pl.multiple_of(s * width, width), width)
        for j in range(1, n_grp // 2):
            there = pl.ds(pl.multiple_of(((s + j) % n_grp) * width, width), width)
            out_ref[here, there] = out_ref[there, here].T
        return carry

    lax.fori_loop(0, n_grp, mirror, 0)


def unpack(parts, table, n_grp):
    width = parts[0].shape[2]
    size = n_grp * width
    return pl.pallas_call(
        functools.partial(unpack_kernel, n_grp),
        in_specs=[SMEM] + [VMEM] * len(parts),
        out_specs=VMEM,
        out_shape=jax.ShapeDtypeStruct((size, size), parts[0].dtype),
        compiler_params=params(),
        cost_estimate=cost(0, 4 * size * size),
        name="unpack",
    )(table, *parts)


def fit_kernel(which, first, has_base, table_ref, metric_ref, *refs):
    refs = list(refs)
    base_ref = refs.pop(0) if has_base else None
    raw_ref = refs.pop()
    out_ref = refs.pop()
    per, width, _ = refs[0].shape
    run = per * width
    high, low = table_ref[which] // per, table_ref[which] % per
    every = len(refs) * run == metric_ref.shape[1]
    blocks = [high ^ (i + first) for i in range(len(refs))]
    for i, group in enumerate(refs):
        for j in range(per):
            row = pl.multiple_of(blocks[i] * run, run) + j * width if every else i * run + j * width
            raw_ref[pl.ds(row, width), :] = group[j ^ low]
    for r in range(0, out_ref.shape[0], TILE):
        rows = slice(r, r + TILE)
        if every:
            total = jnp.dot(metric_ref[rows, :], raw_ref[...], preferred_element_type=F32)
        else:
            total = None
            for i, block in enumerate(blocks):
                cols = pl.ds(pl.multiple_of(block * run, run), run)
                part = jnp.dot(metric_ref[rows, cols], raw_ref[i * run : (i + 1) * run, :], preferred_element_type=F32)
                total = part if total is None else total + part
        if has_base:
            total = total + base_ref[rows, :]
        out_ref[rows, :] = total.astype(out_ref.dtype)


def fit(metric, groups, table, which, first=0, base=None, partial=False):
    size = metric.shape[0]
    per, width, nv = groups[0].shape
    depth = per * width * len(groups)
    given = [metric] + ([base] if base is not None else []) + list(groups)
    return pl.pallas_call(
        functools.partial(fit_kernel, which, first, base is not None),
        in_specs=[SMEM] + [VMEM] * len(given),
        out_specs=VMEM,
        out_shape=jax.ShapeDtypeStruct((size, nv), F32 if partial else BF16),
        scratch_shapes=[pltpu.VMEM((depth, nv), BF16)],
        compiler_params=params(),
        cost_estimate=cost(2 * size * depth * nv, 2 * size * depth),
        name="fit",
    )(table, *given)


def tilde_into(tilde_ref, amp_ref, coulomb_ref, esum, virt_ref):
    nv = amp_ref.shape[0]
    slab = 128
    cuts = range(0, nv, slab)
    for r in cuts:
        mine = jnp.broadcast_to(virt_ref[:, r : r + slab], (slab, slab)).T
        for c in cuts:
            denom = esum - mine - virt_ref[:, c : c + slab]
            amp_ref[r : r + slab, c : c + slab] = coulomb_ref[r : r + slab, c : c + slab] / denom
    energy = jnp.float32(0)
    for r in cuts:
        tilde = 2.0 * amp_ref[r : r + slab, :] - amp_ref[:, r : r + slab].T
        energy += jnp.sum(coulomb_ref[r : r + slab, :] * tilde)
        tilde_ref[r : r + slab, :] = tilde.astype(BF16)
    return energy


def pair_kernel(visits, has_base, final, known, *refs):
    refs = list(refs)
    take = lambda count: [refs.pop(0) for _ in range(count)]
    table_ref, occ_ref, virt_ref, own_ref = take(4)
    others = take(len(visits))
    base_ref = take(1)[0] if has_base else None
    known_refs = take(len(known))
    energy_ref, dens_ref, coulomb_ref, amp_ref = take(4)
    tildes = take(len(visits))
    e_own = occ_ref[table_ref[ORBITAL]]
    for ref, (start, count) in zip(known_refs, known):
        for i in range(count):
            energy_ref[0, start + i] = ref[0, i]
    for at, visit in enumerate(visits):
        coulomb_ref[...] = lax.dot_general(
            own_ref[...], others[at][...], (((0,), (0,)), ((), ())), preferred_element_type=F32
        )
        esum = e_own + occ_ref[table_ref[ORBITAL + visit]]
        energy = tilde_into(tildes[at], amp_ref, coulomb_ref, esum, virt_ref)
        energy_ref[0, visit if final else at] = energy
    if final:
        stage_ref, sems = refs
        ways = own_ref.shape[1] // dens_ref.shape[1]
        copies = []
    for r in range(0, own_ref.shape[0], TILE):
        rows = slice(r, r + TILE)
        total = base_ref[rows, :] if has_base else None
        for other, tilde in zip(others, tildes):
            part = lax.dot_general(
                other[rows, :], tilde[...], (((1,), (1,)), ((), ())), preferred_element_type=F32
            )
            total = part if total is None else total + part
        if final:
            lanes = dens_ref.shape[1]
            for c in range(ways):
                stage_ref[pl.ds(r * ways + c, TILE, stride=ways), :] = total[:, c * lanes : (c + 1) * lanes]
            cut = pl.ds(r * ways, TILE * ways)
            copies.append(pltpu.make_async_copy(stage_ref.at[cut, :], dens_ref.at[cut, :], sems.at[r // TILE]))
            copies[-1].start()
        else:
            dens_ref[rows, :] = total
    if final:
        for copy in copies:
            copy.wait()


def pairs(own, others, visits, table, occ, virt, base=None, final=False, known=()):
    size, nv = own.shape
    lanes = 128
    given = [own, *others] + ([base] if base is not None else [])
    shape = (size * nv // lanes, lanes) if final else (size, nv)
    scratch = [pltpu.VMEM((nv, nv), F32)] * 2 + [pltpu.VMEM((nv, nv), BF16)] * len(visits)
    if final:
        scratch += [pltpu.VMEM(shape, F32), pltpu.SemaphoreType.DMA((size // TILE,))]
    return pl.pallas_call(
        functools.partial(
            pair_kernel, tuple(visits), base is not None, final, tuple((start, count) for start, count, _ in known)
        ),
        in_specs=[SMEM, SMEM, VMEM] + [VMEM] * len(given) + [SMEM] * len(known),
        out_specs=[SMEM, ANY if final else VMEM],
        out_shape=[
            jax.ShapeDtypeStruct((1, VISITS if final else len(visits)), F32),
            jax.ShapeDtypeStruct(shape, F32),
        ],
        scratch_shapes=scratch,
        compiler_params=params(),
        cost_estimate=cost(4 * size * nv * nv * len(visits), 4 * size * nv),
        name="pairs",
    )(table, occ, virt, *given, *(energy for _, _, energy in known))


def body(raw_ints, metric, occ_energy, virt_energy):
    n_grp = lax.axis_size("grp")
    per = n_grp // GROUPS
    g = lax.axis_index("grp")
    table = table_of_integers()

    mine = pack(metric, table, n_grp)
    even = jnp.stack([mine] + [swapped(mine, "grp", k) for k in range(2, n_grp, 2)])
    odd = swapped(even, "grp", 1)
    even_y = swapped(even, "blk", 2)
    odd_y = swapped(odd, "blk", 2)
    parts = [even, odd, swapped(even, "blk", 1), swapped(odd, "blk", 1), even_y, odd_y]
    parts += [swapped(even_y, "blk", 1), swapped(odd_y, "blk", 1)]
    full = unpack(parts, table, n_grp)

    by_orbital = lax.optimization_barrier(jnp.transpose(raw_ints, (1, 0, 2)))
    got = [lax.dynamic_index_in_dim(by_orbital, g ^ k, 0, keepdims=False) for k in range(n_grp)]
    got = got[:1] + [swapped(got[k], "grp", k) for k in range(1, n_grp)]
    groups = [jnp.stack(got[i * per : (i + 1) * per]) for i in range(GROUPS)]
    next_groups = [forwarded(group) for group in groups]

    own = fit(full, groups, table, GRP)
    mate = swapped(own, "blk", 1)
    some = fit(full, next_groups[:-1], table, SOURCE, partial=True)
    next_ = fit(full, next_groups[-1:], table, SOURCE, first=GROUPS - 1, base=some)
    next_mate = swapped(next_, "blk", 1)

    virt = virt_energy[None, :]
    energy_a, base = pairs(own, [own, mate], [0, 1], table, occ_energy, virt)
    energy_b, base = pairs(own, [next_], [2], table, occ_energy, virt, base=base)
    energy, density = pairs(
        own,
        [next_mate],
        [3],
        table,
        occ_energy,
        virt,
        base=base,
        final=True,
        known=[(0, 2, energy_a), (2, 1, energy_b)],
    )
    size, nv = own.shape
    return density.reshape(size, 1, nv), energy


def solution(mesh):
    in_specs = (P("grp", "blk", None), P(None, "grp"), P(), P())
    out_specs = (P(None, ("blk", "grp"), None), P(("blk", "grp"), None))
    return jax.shard_map(body, mesh=mesh, in_specs=in_specs, out_specs=out_specs, check_vma=False)
```

time: 210 us -> 183 us (0.87)
  Pallas kernels: 62.9 us -> 31.5 us
  waiting for transfers between devices: 108 us -> 121 us
  local copies, waits for them, and re-layouts: 7.73 us -> 2.41 us
    pallas_call x6, Pallas kernels: 51.8 us -> 25.4 us  [the longest x3 14.4 us: pairs(): pl.pallas_call(functools.partial(pair_kernel, tuple(visits), base is not...]
    ppermute x4, waiting for transfers between devices: 19.2 us -> 31.3 us  [forwarded(): return lax.ppermute(value, BOTH, pairs)]
    unnamed x35 -> x7, local copies, waits for them, and re-layouts: 7.52 us -> 2.28 us
    pallas_call x1, Pallas kernels: 8.87 us -> 3.92 us  [unpack(): pl.pallas_call(functools.partial(unpack_kernel, n_grp), in_specs=[SMEM] +...]
  transfers between devices with their start and end apart: 23 -> 23, of which waited for: 11 -> 12; matrix products, arithmetic and copies ran while one was open for 2% -> 1% of each run, Pallas kernels for 24% -> 13%
where the time goes in v1:
time: 183 us
  waiting for transfers between devices  121 us (66%)
  Pallas kernels  31.5 us (17%)
  starting transfers between devices  25 us (14%)
  local copies, waits for them, and re-layouts  2.41 us (1%)
    ppermute x19, waiting for transfers between devices, swapped(): return lax.ppermute(value, axis, pairs)  89.9 us
    ppermute x4, waiting for transfers between devices, forwarded(): return lax.ppermute(value, BOTH, pairs)  31.3 us
    ppermute x19, starting transfers between devices, swapped(): return lax.ppermute(value, axis, pairs)  22.4 us
    pallas_call x3, Pallas kernels, pairs(): pl.pallas_call(functools.partial(pair_kernel, tuple(visits), base is not...  14.4 us
    pallas_call x3, Pallas kernels, fit(): pl.pallas_call(functools.partial(fit_kernel, which, first, base is not No...  11 us
    pallas_call x1, Pallas kernels, unpack(): pl.pallas_call(functools.partial(unpack_kernel, n_grp), in_specs=[SMEM] +...  3.92 us
  transfers between devices with their start and end apart: 23, of which 12 were waited for; matrix products, arithmetic and copies ran while one was open for 1% of the time, Pallas kernels for 13%

profile of v1, /device:TPU:17, one launch (start us, length us, event | category | flops | bytes accessed | tf_op | source)
XLA Modules:
  0.0 183.1 jit_solution(3057794765484093948)
XLA Ops:
  1.2 2.2 %pack.1 = bf16[320,256]{1,0:T(8,128)(2,1)} custom-call(s32[8]{0:T(128)} %compare_select_fusion.5.table_ref.refs_0_, bf16[2048,256]{1,0:T(8,128)(2,1)} %metric_ref.1), custom_call_target="tpu_custom_call" | custom-call | tf_op jit(solution)/shard_map/pack/pallas_call | solution.py:75
  3.7 3.2 %collective-permute-start.1 = (bf16[320,256]{1,0:T(8,128)(2,1)}, bf16[320,256]{1,0:T(8,128)(2,1)S(1)}, u32[]{:S(2)}, u32[]{:S(2)}) collective-permute-start(bf16[320,256]{1,0:T(8,128)(2,1)} %pack.1), channel_id=1, source_target_pairs={{0,16},{4,20},{8,24},{12,28},{16,0},{20,4},{24,8},{28,12},{1,17},{... | collective-permute-start | bytes 491528 | tf_op jit(solution)/shard_map/ppermute | solution.py:32
  6.9 8.2 %collective-permute-done.2 = bf16[320,256]{1,0:T(8,128)(2,1)S(1)} collective-permute-done((bf16[320,256]{1,0:T(8,128)(2,1)}, bf16[320,256]{1,0:T(8,128)(2,1)S(1)}, u32[]{:S(2)}, u32[]{:S(2)}) %collective-permute-start.2) | collective-permute-done | bytes 163872 | tf_op jit(solution)/shard_map/ppermute | solution.py:32
  15.1 2.5 %collective-permute-done.1 = bf16[320,256]{1,0:T(8,128)(2,1)S(1)} collective-permute-done((bf16[320,256]{1,0:T(8,128)(2,1)}, bf16[320,256]{1,0:T(8,128)(2,1)S(1)}, u32[]{:S(2)}, u32[]{:S(2)}) %collective-permute-start.1) | collective-permute-done | bytes 163872 | tf_op jit(solution)/shard_map/ppermute | solution.py:32
  19.9 2.3 %copy.9 = bf16[256,8,512]{2,0,1:T(8,128)(2,1)S(1)} copy(bf16[256,8,512]{2,1,0:T(8,128)(2,1)} %param.4) | data formatting | bytes 4194304 | tf_op args[0]
  23.5 10.1 %collective-permute-done.3.refs_1_ = bf16[4,320,256]{2,1,0:T(8,128)(2,1)S(1)} collective-permute-done((bf16[4,320,256]{2,1,0:T(8,128)(2,1)S(1)}, bf16[4,320,256]{2,1,0:T(8,128)(2,1)S(1)}, u32[]{:S(2)}, u32[]{:S(2)}) %collective-permute-start.3) | collective-permute-done | bytes 655392 | tf_op jit(solution)/shard_map/ppermute | solution.py:32
  36.3 2.7 %collective-permute-start.12 = (bf16[256,512]{1,0:T(8,128)(2,1)S(1)}, bf16[256,512]{1,0:T(8,128)(2,1)S(1)}, u32[]{:S(2)}, u32[]{:S(2)}) collective-permute-start(bf16[256,512]{1,0:T(8,128)(2,1)S(1)} %get-tuple-element.20), channel_id=1, source_target_pairs={{0,12},{4,8},{8,4},{12,0},{16,28},{20,24},{24,20},{28,16},{1,13},{... | collective-permute-start | bytes 786440 | tf_op jit(solution)/shard_map/ppermute | solution.py:32
  39.0 4.9 %collective-permute-done.10 = bf16[256,512]{1,0:T(8,128)(2,1)S(1)} collective-permute-done((bf16[256,512]{1,0:T(8,128)(2,1)S(1)}, bf16[256,512]{1,0:T(8,128)(2,1)S(1)}, u32[]{:S(2)}, u32[]{:S(2)}) %collective-permute-start.10) | collective-permute-done | bytes 262176 | tf_op jit(solution)/shard_map/ppermute | solution.py:32
  43.9 7.7 %collective-permute-start.14 = (bf16[256,512]{1,0:T(8,128)(2,1)S(1)}, bf16[256,512]{1,0:T(8,128)(2,1)S(1)}, u32[]{:S(2)}, u32[]{:S(2)}) collective-permute-start(bf16[256,512]{1,0:T(8,128)(2,1)S(1)} %get-tuple-element.18), channel_id=1, source_target_pairs={{0,20},{4,16},{8,28},{12,24},{16,4},{20,0},{24,12},{28,8},{1,21},{... | collective-permute-start | bytes 786440 | tf_op jit(solution)/shard_map/ppermute | solution.py:32
  52.6 20.3 %collective-permute-done.14 = bf16[256,512]{1,0:T(8,128)(2,1)S(1)} collective-permute-done((bf16[256,512]{1,0:T(8,128)(2,1)S(1)}, bf16[256,512]{1,0:T(8,128)(2,1)S(1)}, u32[]{:S(2)}, u32[]{:S(2)}) %collective-permute-start.14) | collective-permute-done | bytes 262176 | tf_op jit(solution)/shard_map/ppermute | solution.py:32
  73.5 5.0 %collective-permute-done.13 = bf16[256,512]{1,0:T(8,128)(2,1)S(1)} collective-permute-done((bf16[256,512]{1,0:T(8,128)(2,1)S(1)}, bf16[256,512]{1,0:T(8,128)(2,1)S(1)}, u32[]{:S(2)}, u32[]{:S(2)}) %collective-permute-start.13) | collective-permute-done | bytes 262176 | tf_op jit(solution)/shard_map/ppermute | solution.py:32
  79.6 5.3 %collective-permute-done.16 = bf16[256,512]{1,0:T(8,128)(2,1)S(1)} collective-permute-done((bf16[256,512]{1,0:T(8,128)(2,1)S(1)}, bf16[256,512]{1,0:T(8,128)(2,1)S(1)}, u32[]{:S(2)}, u32[]{:S(2)}) %collective-permute-start.16) | collective-permute-done | bytes 262176 | tf_op jit(solution)/shard_map/ppermute | solution.py:32
  85.7 33.5 %collective-permute-done.15 = bf16[256,512]{1,0:T(8,128)(2,1)S(1)} collective-permute-done((bf16[256,512]{1,0:T(8,128)(2,1)S(1)}, bf16[256,512]{1,0:T(8,128)(2,1)S(1)}, u32[]{:S(2)}, u32[]{:S(2)}) %collective-permute-start.15) | collective-permute-done | bytes 262176 | tf_op jit(solution)/shard_map/ppermute | solution.py:32
  119.4 2.6 %collective-permute-start.20 = (bf16[2,256,512]{2,1,0:T(8,128)(2,1)S(1)}, bf16[2,256,512]{2,1,0:T(8,128)(2,1)S(1)}, u32[]{:S(2)}, u32[]{:S(2)}) collective-permute-start(bf16[2,256,512]{2,1,0:T(8,128)(2,1)S(1)} %pad_maximum_fusion.4.refs_3_), channel_id=1, source_target_pairs={{0,2},{1,31},{2,4},{3,1},{4,6},{5,3},{6,8},{7,5},{8,10},{9,7},{10,... | collective-permute-start | bytes 1572872 | tf_op jit(solution)/shard_map/ppermute | solution.py:38
  122.0 3.9 %unpack.1.metric_ref = bf16[2048,2048]{1,0:T(8,128)(2,1)S(1)} custom-call(s32[8]{0:T(128)S(1)} %copy-done, bf16[4,320,256]{2,1,0:T(8,128)(2,1)S(1)} %pad_maximum_fusion.refs_0_, bf16[4,320,256]{2,1,0:T(8,128)(2,1)S(1)} %collective-permute-done.3.refs_1_, bf16[4,320,256]{2,1,0:T(8,128)(2,1)S(1)} %collective-permute-done.4.refs_2_, ...), custom_call_target="tpu_custom_call" | custom-call | bytes 16777216 | tf_op jit(solution)/shard_map/unpack/pallas_call | solution.py:117
  125.9 5.2 %fit.3.refs_3_.refs_4_ = bf16[2048,512]{1,0:T(8,128)(2,1)S(1)} custom-call(s32[8]{0:T(128)S(1)} %copy-done, bf16[2048,2048]{1,0:T(8,128)(2,1)S(1)} %unpack.1.metric_ref, bf16[2,256,512]{2,1,0:T(8,128)(2,1)S(1)} %pad_maximum_fusion.1.refs_0_, bf16[2,256,512]{2,1,0:T(8,128)(2,1)S(1)} %pad_maximum_fusion.2.refs_1_, ...), custom_call_target="tpu_custom_call" | custom-call | flops 4294967296 | bytes 8388608 | tf_op jit(solution)/shard_map/fit/pallas_call | solution.py:162
  131.3 18.5 %collective-permute-done.17.refs_0_ = bf16[2,256,512]{2,1,0:T(8,128)(2,1)S(1)} collective-permute-done((bf16[2,256,512]{2,1,0:T(8,128)(2,1)S(1)}, bf16[2,256,512]{2,1,0:T(8,128)(2,1)S(1)}, u32[]{:S(2)}, u32[]{:S(2)}) %collective-permute-start.17) | collective-permute-done | bytes 524320 | tf_op jit(solution)/shard_map/ppermute | solution.py:38
  149.7 5.6 %collective-permute-done.18.refs_1_ = bf16[2,256,512]{2,1,0:T(8,128)(2,1)S(1)} collective-permute-done((bf16[2,256,512]{2,1,0:T(8,128)(2,1)S(1)}, bf16[2,256,512]{2,1,0:T(8,128)(2,1)S(1)}, u32[]{:S(2)}, u32[]{:S(2)}) %collective-permute-start.18) | collective-permute-done | bytes 524320 | tf_op jit(solution)/shard_map/ppermute | solution.py:38
  155.3 5.6 %collective-permute-done.19.refs_2_ = bf16[2,256,512]{2,1,0:T(8,128)(2,1)S(1)} collective-permute-done((bf16[2,256,512]{2,1,0:T(8,128)(2,1)S(1)}, bf16[2,256,512]{2,1,0:T(8,128)(2,1)S(1)}, u32[]{:S(2)}, u32[]{:S(2)}) %collective-permute-start.19) | collective-permute-done | bytes 524320 | tf_op jit(solution)/shard_map/ppermute | solution.py:38
  160.9 4.0 %fit.4.refs_0_ = f32[2048,512]{1,0:T(8,128)S(1)} custom-call(s32[8]{0:T(128)S(1)} %copy-done, bf16[2048,2048]{1,0:T(8,128)(2,1)S(1)} %unpack.1.metric_ref, bf16[2,256,512]{2,1,0:T(8,128)(2,1)S(1)} %collective-permute-done.17.refs_0_, bf16[2,256,512]{2,1,0:T(8,128)(2,1)S(1)} %collective-permute-done.18.refs_1_, ...), custom_call_target="tpu_custom_call" | custom-call | flops 3221225472 | bytes 6291456 | tf_op jit(solution)/shard_map/fit/pallas_call | solution.py:162
  166.6 1.8 fit.5.refs_4_
  168.5 5.6 %pairs.3 = (f32[1,2]{1,0:T(1,128)S(1)}, f32[2048,512]{1,0:T(8,128)S(1)}) custom-call(s32[8]{0:T(128)S(1)} %copy-done, f32[32]{0:T(128)S(1)} %copy-done.2, f32[1,512]{1,0:T(1,128)S(1)} %bitcast.30, bf16[2048,512]{1,0:T(8,128)(2,1)S(1)} %fit.3.refs_3_.refs_4_, bf16[2048,512]{1,0:T(8,128)(2,1)S(1)} %fit.3.refs_3_.refs_4_, ...), custom_call_target="tpu_custom_call" | custom-call | flops 4294967296 | bytes 4194304 | tf_op jit(solution)/shard_map/pairs/pallas_call | solution.py:245
  174.1 3.2 %pairs.4 = (f32[1,1]{1,0:T(1,128)}, f32[2048,512]{1,0:T(8,128)S(1)}) custom-call(s32[8]{0:T(128)S(1)} %copy-done, f32[32]{0:T(128)S(1)} %copy-done.2, f32[1,512]{1,0:T(1,128)S(1)} %bitcast.31, bf16[2048,512]{1,0:T(8,128)(2,1)S(1)} %fit.3.refs_3_.refs_4_, bf16[2048,512]{1,0:T(8,128)(2,1)S(1)} %fit.5.refs_4_, f32[2048,512]{1,0:T(8,128)S(1)} %get-tuple-element.8.refs_5_), custom_call_target="tpu_custom_call" | custom-call | flops 2147483648 | bytes 4194304 | tf_op jit(solution)/shard_map/pairs/pallas_call | solution.py:245
  177.3 5.5 %pairs.5 = (f32[1,4]{1,0:T(1,128)}, f32[8192,128]{1,0:T(8,128)}) custom-call(s32[8]{0:T(128)S(1)} %copy-done, f32[32]{0:T(128)S(1)} %copy-done.2, f32[1,512]{1,0:T(1,128)S(1)} %bitcast.32, bf16[2048,512]{1,0:T(8,128)(2,1)S(1)} %fit.3.refs_3_.refs_4_, bf16[2048,512]{1,0:T(8,128)(2,1)S(1)} %collective-permute-done.21.refs_4_, ...), custom_call_target="tpu_custom_call" | custom-call | flops 2147483648 | bytes 4194304 | tf_op jit(solution)/shard_map/pairs/pallas_call | solution.py:245
  (44 shorter events, 12.4 us)
Async XLA Ops:
  3.4 11.7 %collective-permute-start.2 = (bf16[320,256]{1,0:T(8,128)(2,1)}, bf16[320,256]{1,0:T(8,128)(2,1)S(1)}, u32[]{:S(2)}, u32[]{:S(2)}) collective-permute-start(bf16[320,256]{1,0:T(8,128)(2,1)} %pack.1), channel_id=1, source_target_pairs={{0,24},{4,28},{8,16},{12,20},{16,8},{20,12},{24,0},{28,4},{1,25},{... | collective-permute-start | bytes 491528 | tf_op jit(solution)/shard_map/ppermute | solution.py:32
  3.7 13.9 %collective-permute-start.1 = (bf16[320,256]{1,0:T(8,128)(2,1)}, bf16[320,256]{1,0:T(8,128)(2,1)S(1)}, u32[]{:S(2)}, u32[]{:S(2)}) collective-permute-start(bf16[320,256]{1,0:T(8,128)(2,1)} %pack.1), channel_id=1, source_target_pairs={{0,16},{4,20},{8,24},{12,28},{16,0},{20,4},{24,8},{28,12},{1,17},{... | collective-permute-start | bytes 491528 | tf_op jit(solution)/shard_map/ppermute | solution.py:32
  6.9 10.7 %collective-permute-start = (bf16[320,256]{1,0:T(8,128)(2,1)}, bf16[320,256]{1,0:T(8,128)(2,1)S(1)}, u32[]{:S(2)}, u32[]{:S(2)}) collective-permute-start(bf16[320,256]{1,0:T(8,128)(2,1)} %pack.1), channel_id=1, source_target_pairs={{0,8},{4,12},{8,0},{12,4},{16,24},{20,28},{24,16},{28,20},{1,9},{5... | collective-permute-start | bytes 491528 | tf_op jit(solution)/shard_map/ppermute | solution.py:32
  18.6 15.0 %collective-permute-start.3 = (bf16[4,320,256]{2,1,0:T(8,128)(2,1)S(1)}, bf16[4,320,256]{2,1,0:T(8,128)(2,1)S(1)}, u32[]{:S(2)}, u32[]{:S(2)}) collective-permute-start(bf16[4,320,256]{2,1,0:T(8,128)(2,1)S(1)} %pad_maximum_fusion.refs_0_), channel_id=1, source_target_pairs={{0,4},{4,0},{8,12},{12,8},{16,20},{20,16},{24,28},{28,24},{1,5},{5... | collective-permute-start | bytes 1966088 | tf_op jit(solution)/shard_map/ppermute | solution.py:32
  22.2 56.9 %collective-permute-start.6 = (bf16[4,320,256]{2,1,0:T(8,128)(2,1)S(1)}, bf16[4,320,256]{2,1,0:T(8,128)(2,1)S(1)}, u32[]{:S(2)}, u32[]{:S(2)}) collective-permute-start(bf16[4,320,256]{2,1,0:T(8,128)(2,1)S(1)} %pad_maximum_fusion.refs_0_), channel_id=1, source_target_pairs={{0,2},{1,3},{2,0},{3,1},{4,6},{5,7},{6,4},{7,5},{8,10},{9,11},{10,... | collective-permute-start | bytes 1966088 | tf_op jit(solution)/shard_map/ppermute | solution.py:32
  33.6 45.5 %collective-permute-start.7 = (bf16[4,320,256]{2,1,0:T(8,128)(2,1)S(1)}, bf16[4,320,256]{2,1,0:T(8,128)(2,1)S(1)}, u32[]{:S(2)}, u32[]{:S(2)}) collective-permute-start(bf16[4,320,256]{2,1,0:T(8,128)(2,1)S(1)} %collective-permute-done.3.refs_1_), channel_id=1, source_target_pairs={{0,2},{1,3},{2,0},{3,1},{4,6},{5,7},{6,4},{7,5},{8,10},{9,11},{10,... | collective-permute-start | bytes 1966088 | tf_op jit(solution)/shard_map/ppermute | solution.py:32
  35.0 8.9 %collective-permute-start.10 = (bf16[256,512]{1,0:T(8,128)(2,1)S(1)}, bf16[256,512]{1,0:T(8,128)(2,1)S(1)}, u32[]{:S(2)}, u32[]{:S(2)}) collective-permute-start(bf16[256,512]{1,0:T(8,128)(2,1)S(1)} %get-tuple-element.22), channel_id=1, source_target_pairs={{0,4},{4,0},{8,12},{12,8},{16,20},{20,16},{24,28},{28,24},{1,5},{5... | collective-permute-start | bytes 786440 | tf_op jit(solution)/shard_map/ppermute | solution.py:32
  36.3 15.4 %collective-permute-start.12 = (bf16[256,512]{1,0:T(8,128)(2,1)S(1)}, bf16[256,512]{1,0:T(8,128)(2,1)S(1)}, u32[]{:S(2)}, u32[]{:S(2)}) collective-permute-start(bf16[256,512]{1,0:T(8,128)(2,1)S(1)} %get-tuple-element.20), channel_id=1, source_target_pairs={{0,12},{4,8},{8,4},{12,0},{16,28},{20,24},{24,20},{28,16},{1,13},{... | collective-permute-start | bytes 786440 | tf_op jit(solution)/shard_map/ppermute | solution.py:32
  39.0 12.7 %collective-permute-start.11 = (bf16[256,512]{1,0:T(8,128)(2,1)S(1)}, bf16[256,512]{1,0:T(8,128)(2,1)S(1)}, u32[]{:S(2)}, u32[]{:S(2)}) collective-permute-start(bf16[256,512]{1,0:T(8,128)(2,1)S(1)} %get-tuple-element.21), channel_id=1, source_target_pairs={{0,8},{4,12},{8,0},{12,4},{16,24},{20,28},{24,16},{28,20},{1,9},{5... | collective-permute-start | bytes 786440 | tf_op jit(solution)/shard_map/ppermute | solution.py:32
  43.9 29.0 %collective-permute-start.14 = (bf16[256,512]{1,0:T(8,128)(2,1)S(1)}, bf16[256,512]{1,0:T(8,128)(2,1)S(1)}, u32[]{:S(2)}, u32[]{:S(2)}) collective-permute-start(bf16[256,512]{1,0:T(8,128)(2,1)S(1)} %get-tuple-element.18), channel_id=1, source_target_pairs={{0,20},{4,16},{8,28},{12,24},{16,4},{20,0},{24,12},{28,8},{1,21},{... | collective-permute-start | bytes 786440 | tf_op jit(solution)/shard_map/ppermute | solution.py:32
  51.7 26.8 %collective-permute-start.13 = (bf16[256,512]{1,0:T(8,128)(2,1)S(1)}, bf16[256,512]{1,0:T(8,128)(2,1)S(1)}, u32[]{:S(2)}, u32[]{:S(2)}) collective-permute-start(bf16[256,512]{1,0:T(8,128)(2,1)S(1)} %get-tuple-element.19), channel_id=1, source_target_pairs={{0,16},{4,20},{8,24},{12,28},{16,0},{20,4},{24,8},{28,12},{1,17},{... | collective-permute-start | bytes 786440 | tf_op jit(solution)/shard_map/ppermute | solution.py:32
  51.7 33.3 %collective-permute-start.16 = (bf16[256,512]{1,0:T(8,128)(2,1)S(1)}, bf16[256,512]{1,0:T(8,128)(2,1)S(1)}, u32[]{:S(2)}, u32[]{:S(2)}) collective-permute-start(bf16[256,512]{1,0:T(8,128)(2,1)S(1)} %get-tuple-element.17), channel_id=1, source_target_pairs={{0,28},{4,24},{8,20},{12,16},{16,12},{20,8},{24,4},{28,0},{1,29},{... | collective-permute-start | bytes 786440 | tf_op jit(solution)/shard_map/ppermute | solution.py:32
  72.9 46.4 %collective-permute-start.4 = (bf16[4,320,256]{2,1,0:T(8,128)(2,1)S(1)}, bf16[4,320,256]{2,1,0:T(8,128)(2,1)S(1)}, u32[]{:S(2)}, u32[]{:S(2)}) collective-permute-start(bf16[4,320,256]{2,1,0:T(8,128)(2,1)S(1)} %pad_maximum_fusion.refs_0_), channel_id=1, source_target_pairs={{0,1},{1,0},{2,3},{3,2},{4,5},{5,4},{6,7},{7,6},{8,9},{9,8},{10,11... | collective-permute-start | bytes 1966088 | tf_op jit(solution)/shard_map/ppermute | solution.py:32
  78.5 40.8 %collective-permute-start.5 = (bf16[4,320,256]{2,1,0:T(8,128)(2,1)S(1)}, bf16[4,320,256]{2,1,0:T(8,128)(2,1)S(1)}, u32[]{:S(2)}, u32[]{:S(2)}) collective-permute-start(bf16[4,320,256]{2,1,0:T(8,128)(2,1)S(1)} %collective-permute-done.3.refs_1_), channel_id=1, source_target_pairs={{0,1},{1,0},{2,3},{3,2},{4,5},{5,4},{6,7},{7,6},{8,9},{9,8},{10,11... | collective-permute-start | bytes 1966088 | tf_op jit(solution)/shard_map/ppermute | solution.py:32
  79.1 40.3 %collective-permute-start.8 = (bf16[4,320,256]{2,1,0:T(8,128)(2,1)S(1)}, bf16[4,320,256]{2,1,0:T(8,128)(2,1)S(1)}, u32[]{:S(2)}, u32[]{:S(2)}) collective-permute-start(bf16[4,320,256]{2,1,0:T(8,128)(2,1)S(1)} %collective-permute-done.6.refs_4_), channel_id=1, source_target_pairs={{0,1},{1,0},{2,3},{3,2},{4,5},{5,4},{6,7},{7,6},{8,9},{9,8},{10,11... | collective-permute-start | bytes 1966088 | tf_op jit(solution)/shard_map/ppermute | solution.py:32
  79.1 42.9 %collective-permute-start.9 = (bf16[4,320,256]{2,1,0:T(8,128)(2,1)S(1)}, bf16[4,320,256]{2,1,0:T(8,128)(2,1)S(1)}, u32[]{:S(2)}, u32[]{:S(2)}) collective-permute-start(bf16[4,320,256]{2,1,0:T(8,128)(2,1)S(1)} %collective-permute-done.7.refs_5_), channel_id=1, source_target_pairs={{0,1},{1,0},{2,3},{3,2},{4,5},{5,4},{6,7},{7,6},{8,9},{9,8},{10,11... | collective-permute-start | bytes 1966088 | tf_op jit(solution)/shard_map/ppermute | solution.py:32
  84.9 34.3 %collective-permute-start.15 = (bf16[256,512]{1,0:T(8,128)(2,1)S(1)}, bf16[256,512]{1,0:T(8,128)(2,1)S(1)}, u32[]{:S(2)}, u32[]{:S(2)}) collective-permute-start(bf16[256,512]{1,0:T(8,128)(2,1)S(1)} %get-tuple-element.16), channel_id=1, source_target_pairs={{0,24},{4,28},{8,16},{12,20},{16,8},{20,12},{24,0},{28,4},{1,25},{... | collective-permute-start | bytes 786440 | tf_op jit(solution)/shard_map/ppermute | solution.py:32
  85.5 36.5 %copy-start = (s32[8]{0:T(128)S(1)}, s32[8]{0:T(128)}, u32[]{:S(2)}) copy-start(s32[8]{0:T(128)} %compare_select_fusion.5.table_ref.refs_0_) | copy-start | bytes 100
  119.2 30.5 %collective-permute-start.17 = (bf16[2,256,512]{2,1,0:T(8,128)(2,1)S(1)}, bf16[2,256,512]{2,1,0:T(8,128)(2,1)S(1)}, u32[]{:S(2)}, u32[]{:S(2)}) collective-permute-start(bf16[2,256,512]{2,1,0:T(8,128)(2,1)S(1)} %pad_maximum_fusion.1.refs_0_), channel_id=1, source_target_pairs={{0,2},{1,31},{2,4},{3,1},{4,6},{5,3},{6,8},{7,5},{8,10},{9,7},{10,... | collective-permute-start | bytes 1572872 | tf_op jit(solution)/shard_map/ppermute | solution.py:38
  119.3 36.1 %collective-permute-start.18 = (bf16[2,256,512]{2,1,0:T(8,128)(2,1)S(1)}, bf16[2,256,512]{2,1,0:T(8,128)(2,1)S(1)}, u32[]{:S(2)}, u32[]{:S(2)}) collective-permute-start(bf16[2,256,512]{2,1,0:T(8,128)(2,1)S(1)} %pad_maximum_fusion.2.refs_1_), channel_id=1, source_target_pairs={{0,2},{1,31},{2,4},{3,1},{4,6},{5,3},{6,8},{7,5},{8,10},{9,7},{10,... | collective-permute-start | bytes 1572872 | tf_op jit(solution)/shard_map/ppermute | solution.py:38
  119.3 41.6 %collective-permute-start.19 = (bf16[2,256,512]{2,1,0:T(8,128)(2,1)S(1)}, bf16[2,256,512]{2,1,0:T(8,128)(2,1)S(1)}, u32[]{:S(2)}, u32[]{:S(2)}) collective-permute-start(bf16[2,256,512]{2,1,0:T(8,128)(2,1)S(1)} %pad_maximum_fusion.3.refs_2_), channel_id=1, source_target_pairs={{0,2},{1,31},{2,4},{3,1},{4,6},{5,3},{6,8},{7,5},{8,10},{9,7},{10,... | collective-permute-start | bytes 1572872 | tf_op jit(solution)/shard_map/ppermute | solution.py:38
  119.4 47.1 %collective-permute-start.20 = (bf16[2,256,512]{2,1,0:T(8,128)(2,1)S(1)}, bf16[2,256,512]{2,1,0:T(8,128)(2,1)S(1)}, u32[]{:S(2)}, u32[]{:S(2)}) collective-permute-start(bf16[2,256,512]{2,1,0:T(8,128)(2,1)S(1)} %pad_maximum_fusion.4.refs_3_), channel_id=1, source_target_pairs={{0,2},{1,31},{2,4},{3,1},{4,6},{5,3},{6,8},{7,5},{8,10},{9,7},{10,... | collective-permute-start | bytes 1572872 | tf_op jit(solution)/shard_map/ppermute | solution.py:38
  131.2 37.3 %collective-permute-start.22 = (bf16[2048,512]{1,0:T(8,128)(2,1)S(1)}, bf16[2048,512]{1,0:T(8,128)(2,1)S(1)}, u32[]{:S(2)}, u32[]{:S(2)}) collective-permute-start(bf16[2048,512]{1,0:T(8,128)(2,1)S(1)} %fit.3.refs_3_.refs_4_), channel_id=1, source_target_pairs={{0,1},{1,0},{2,3},{3,2},{4,5},{5,4},{6,7},{7,6},{8,9},{9,8},{10,11... | collective-permute-start | bytes 6291464 | tf_op jit(solution)/shard_map/ppermute | solution.py:32
  168.4 9.0 %collective-permute-start.21 = (bf16[2048,512]{1,0:T(8,128)(2,1)S(1)}, bf16[2048,512]{1,0:T(8,128)(2,1)S(1)}, u32[]{:S(2)}, u32[]{:S(2)}) collective-permute-start(bf16[2048,512]{1,0:T(8,128)(2,1)S(1)} %fit.5.refs_4_), channel_id=1, source_target_pairs={{0,1},{1,0},{2,3},{3,2},{4,5},{5,4},{6,7},{7,6},{8,9},{9,8},{10,11... | collective-permute-start | bytes 6291464 | tf_op jit(solution)/shard_map/ppermute | solution.py:32
  (2 other events, 7.1 us)
